TPU v7x, 512 devices: a whole 4x4x16 slice. The times are simulated.
512 devices in a mesh: ctx: 8 (over y, z_hi), tp: 64 (over x, z_lo, core).
Axes of the slice: x: 4, y: 4, z: 16 (z_hi: 2, z_lo: 8; z = z_hi * 8 + z_lo), core: 2. Of those that a mesh axis runs over, the one named last changes fastest.
Arguments:
- hidden: bfloat16 [2048, 2048], P(('ctx', 'tp')), may hold values from -6 to 6
- w_in: bfloat16 [2048, 8192], P(None, 'tp'), may hold values from -0.125 to 0.125
- w_bc: bfloat16 [2048, 32], replicated, may hold values from -0.125 to 0.125
- w_dt: bfloat16 [64, 2048], P('tp'), may hold values from -0.125 to 0.125
- dt_bias: float32 [64], P('tp'), may hold values from -5 to -3
- a_log: float32 [64], P('tp'), may hold values from -4.6 to 0
- d_skip: float32 [64], P('tp'), may hold values from 0.5 to 1.5
- conv_w: float32 [4, 4096], P(None, 'tp'), may hold values from -3 to 3
- w_out: bfloat16 [4096, 2048], P('tp'), may hold values from -0.09375 to 0.09375
- d_out: bfloat16 [2048, 2048], P(('ctx', 'tp')), may hold values from -6 to 6
Outputs:
- d_hidden: bfloat16 [2048, 2048], P(('ctx', 'tp'))
- d_w_in: float32 [2048, 8192], P(None, 'tp')
- d_w_out: float32 [4096, 2048], P('tp')
- d_w_bc: float32 [2048, 32], replicated
All inputs are finite; a program needn't handle non-finite values.
Results may differ from a plain program's by a relative error of at most 0.017.
Values may be sent and summed in bfloat16 or wider, within the bound.
A program may use at most 64 MiB of HBM per device.

v0:
```python
import math
import jax
import jax.numpy as jnp
from jax import lax
from jax.sharding import PartitionSpec as P

STATE = 16
CONV = 4
precise = lax.Precision.HIGHEST


def padded(array, sides, width):
    for axis, dim in sides:
        size, length = (lax.axis_size(axis), array.shape[dim])
        up = [(i, (i + 1) % size) for i in range(size - 1)]
        down = [(j, i) for i, j in up]
        last = lax.slice_in_dim(array, length - width, length, axis=dim)
        leading = lax.slice_in_dim(array, 0, width, axis=dim)
        before = lax.ppermute(last, axis, up)
        after = lax.ppermute(leading, axis, down)
        array = jnp.concatenate([before, array, after], axis=dim)
    return array


def entering(array, axis, combine, identity, reverse):
    length, index = (lax.axis_size(axis), lax.axis_index(axis))
    everything = jax.tree.map(lambda part: lax.all_gather(part, axis), array)
    start = jax.tree.map(
        lambda part, zero: jnp.broadcast_to(jnp.asarray(zero, part.dtype), part.shape),
        array,
        identity,
    )

    def step(k, before):
        at = length - 1 - k if reverse else k
        reached = at > index if reverse else at < index
        new = combine(before, jax.tree.map(lambda part: part[at], everything))
        return jax.tree.map(lambda a, b: jnp.where(reached, a, b), new, before)

    return lax.fori_loop(0, length, step, start)


def times_rows(operand_a, operand_b):
    return lax.dot_general(
        operand_a, operand_b, (((1,), (1,)), ((), ())), preferred_element_type=jnp.float32
    )


def across_rows(operand_a, operand_b):
    return lax.dot_general(
        operand_a, operand_b, (((0,), (0,)), ((), ())), preferred_element_type=jnp.float32
    )


def conv_silu(x_ext, conv_w):
    length = x_ext.shape[0] - CONV + 1
    summed = conv_w[0] * x_ext[0:length]
    for shift_k in range(1, CONV):
        summed = summed + conv_w[shift_k] * x_ext[shift_k : shift_k + length]
    return jax.nn.silu(summed)


def block_ssd(conv_out, steps_dt, b_rows, c_rows, decay_rate, state_in):
    positions = conv_out.shape[0]
    log_keep = jnp.cumsum(steps_dt * decay_rate)
    causal = lax.broadcasted_iota(jnp.int32, (positions, positions), 0) >= lax.broadcasted_iota(
        jnp.int32, (positions, positions), 1
    )
    decays = jnp.exp(jnp.where(causal, log_keep[:, None] - log_keep[None, :], -jnp.inf))
    scores = jnp.einsum("in,jn->ij", c_rows, b_rows, precision=precise) * decays
    weighted = steps_dt[:, None] * conv_out
    outputs = jnp.einsum("ij,jp->ip", scores, weighted, precision=precise)
    outputs = outputs + jnp.exp(log_keep)[:, None] * jnp.einsum(
        "in,pn->ip", c_rows, state_in, precision=precise
    )
    remains = jnp.exp(log_keep[-1] - log_keep)
    state_out = jnp.exp(log_keep[-1]) * state_in + jnp.einsum(
        "j,jp,jn->pn", remains, weighted, b_rows, precision=precise
    )
    return (outputs, state_out)


def strand_core(x_ext, gate_in, b_c, dt_raw, state_in, params):
    dt_bias_h, decay_rate, skip_h, conv_w = params
    conv_out = conv_silu(x_ext, conv_w)
    steps_dt = jax.nn.softplus(dt_raw + dt_bias_h)
    outputs, state_out = block_ssd(
        conv_out, steps_dt, b_c[:, :STATE], b_c[:, STATE:], decay_rate, state_in
    )
    gated = (outputs + skip_h * conv_out) * jax.nn.silu(gate_in)
    return (gated, state_out)


def strand_summary(x_ext, b_c, dt_raw, params):
    dt_bias_h, decay_rate, skip_h, conv_w = params
    conv_out = conv_silu(x_ext, conv_w)
    steps_dt = jax.nn.softplus(dt_raw + dt_bias_h)
    log_keep = jnp.cumsum(steps_dt * decay_rate)
    remains = jnp.exp(log_keep[-1] - log_keep) * steps_dt
    local_state = jnp.einsum("j,jp,jn->pn", remains, conv_out, b_c[:, :STATE], precision=precise)
    return (jnp.exp(log_keep[-1]), local_state)


def chain_step(earlier, following):
    return (earlier[0] * following[0], following[0] * earlier[1] + following[1])


def local(hidden, w_in, w_bc, w_dt, dt_bias, a_log, d_skip, conv_w, w_out, d_out):
    own_rows = hidden.shape[0]
    seq_rows = own_rows * lax.axis_size("tp")
    length_all = seq_rows * lax.axis_size("ctx")
    head_dim = w_out.shape[0]
    rim_rows = CONV - 1
    w_pair = jnp.concatenate([w_in, w_in[::-1]], axis=1)
    bc_pair = jnp.concatenate([w_bc, w_bc[::-1]], axis=1)
    dt_pair = jnp.concatenate([w_dt, w_dt[:, ::-1]], axis=0)
    out_pair = jnp.concatenate([w_out, w_out[:, ::-1]], axis=0)
    params = (dt_bias[0], -jnp.exp(a_log[0]), d_skip[0], conv_w)
    gathered = lax.all_gather(hidden, "tp", axis=0, tiled=True)
    projected = jnp.dot(gathered, w_pair, preferred_element_type=jnp.float32).astype(jnp.bfloat16)
    dt_raw = times_rows(gathered, dt_pair)
    b_c_all = jnp.dot(gathered, bc_pair, preferred_element_type=jnp.float32)
    x_both = jnp.concatenate(
        [projected[:, :head_dim], projected[:, 2 * head_dim : 3 * head_dim]], axis=1
    )
    x_halo = padded(x_both, (("ctx", 0),), rim_rows).astype(jnp.float32)
    x_ext = jnp.stack(
        [x_halo[: seq_rows + rim_rows, :head_dim], x_halo[rim_rows:, head_dim:][::-1]]
    )
    gate_in = jnp.stack(
        [projected[:, head_dim : 2 * head_dim], projected[::-1, 3 * head_dim :]]
    ).astype(jnp.float32)
    b_c = jnp.stack([b_c_all[:, : 2 * STATE], b_c_all[::-1, 2 * STATE :]])
    dt_both = jnp.stack([dt_raw[:, 0], dt_raw[::-1, 1]])
    decays, local_states = jax.vmap(strand_summary, in_axes=(0, 0, 0, None))(
        x_ext, b_c, dt_both, params
    )
    identity = (jnp.ones((), jnp.float32), jnp.zeros((head_dim, STATE), jnp.float32))
    fwd_in = entering((decays[0], local_states[0]), "ctx", chain_step, identity, False)[1]
    rev_in = entering((decays[1], local_states[1]), "ctx", chain_step, identity, True)[1]
    states_in = jnp.stack([fwd_in, rev_in])

    def core_both(x_part, gate_part, bc_part, dt_part, state_part):
        return jax.vmap(strand_core, in_axes=(0, 0, 0, 0, 0, None))(
            x_part, gate_part, bc_part, dt_part, state_part, params
        )

    (gated, states_out), pullback = jax.vjp(core_both, x_ext, gate_in, b_c, dt_both, states_in)
    gated_nat = jnp.concatenate([gated[0], gated[1][::-1]], axis=1).astype(jnp.bfloat16)
    portion = lax.all_gather(d_out, "tp", axis=0, tiled=True)
    grads_g = times_rows(portion, out_pair)
    grad_wout = across_rows(gated_nat, portion)
    grad_stack = jnp.stack([grads_g[:, :head_dim], grads_g[::-1, head_dim:]])
    direct = pullback((grad_stack, jnp.zeros_like(states_out)))
    direct_state = direct[4]
    fwd_adj = entering((decays[0], direct_state[0]), "ctx", chain_step, identity, True)[1]
    rev_adj = entering((decays[1], direct_state[1]), "ctx", chain_step, identity, False)[1]
    carried_grads = pullback((jnp.zeros_like(gated), jnp.stack([fwd_adj, rev_adj])))
    grad_x = direct[0] + carried_grads[0]
    grad_gates = direct[1] + carried_grads[1]
    grad_bcs = direct[2] + carried_grads[2]
    grad_dts = direct[3] + carried_grads[3]
    grad_x_rev = grad_x[1][::-1]
    grad_x_local = jnp.concatenate([grad_x[0][rim_rows:], grad_x_rev[:seq_rows]], axis=1)
    outgoing = jnp.concatenate([grad_x[0][:rim_rows], grad_x_rev[seq_rows:]], axis=0)
    incoming = padded(outgoing, (("ctx", 0),), rim_rows)
    grad_x_local = grad_x_local.at[:rim_rows, head_dim:].add(incoming[:rim_rows])
    grad_x_local = grad_x_local.at[seq_rows - rim_rows :, :head_dim].add(incoming[3 * rim_rows :])
    grad_proj = jnp.concatenate(
        [
            grad_x_local[:, :head_dim],
            grad_gates[0],
            grad_x_local[:, head_dim:],
            grad_gates[1][::-1],
        ],
        axis=1,
    ).astype(jnp.bfloat16)
    grad_bc = jnp.concatenate([grad_bcs[0], grad_bcs[1][::-1]], axis=1).astype(jnp.bfloat16)
    grad_dt = jnp.stack([grad_dts[0], grad_dts[1][::-1]], axis=1).astype(jnp.bfloat16)

    def strand_term(which):
        proj_cols = grad_proj[:, which * 2 * head_dim : (which + 1) * 2 * head_dim]
        wide_cols = w_pair[:, which * 2 * head_dim : (which + 1) * 2 * head_dim]
        bc_cols = grad_bc[:, which * 2 * STATE : (which + 1) * 2 * STATE]
        shared_cols = bc_pair[:, which * 2 * STATE : (which + 1) * 2 * STATE]
        dt_cols = grad_dt[:, which : which + 1]
        dt_rows = dt_pair[which : which + 1]
        summed = times_rows(proj_cols, wide_cols) + times_rows(bc_cols, shared_cols)
        return summed + jnp.dot(dt_cols, dt_rows, preferred_element_type=jnp.float32)

    forward_part = lax.psum_scatter(strand_term(0), "tp", scatter_dimension=0, tiled=True)
    reverse_part = lax.psum_scatter(strand_term(1), "tp", scatter_dimension=0, tiled=True)
    d_hidden = (forward_part + reverse_part).astype(jnp.bfloat16)
    scaling = 1.0 / math.sqrt(length_all)
    grad_pair = across_rows(gathered, grad_proj)
    d_w_in = (grad_pair[:, : 2 * head_dim] + grad_pair[::-1, 2 * head_dim :]) * scaling
    d_w_out = (grad_wout[:head_dim] + grad_wout[head_dim:, ::-1]) * scaling
    d_w_in, d_w_out = (
        lax.psum(d_w_in.astype(jnp.bfloat16), "ctx").astype(jnp.float32),
        lax.psum(d_w_out.astype(jnp.bfloat16), "ctx").astype(jnp.float32),
    )
    grad_bpair = across_rows(gathered, grad_bc)
    d_w_bc = lax.psum(
        (grad_bpair[:, : 2 * STATE] + grad_bpair[::-1, 2 * STATE :]) * scaling, ("ctx", "tp")
    )
    return (d_hidden, d_w_in, d_w_out, d_w_bc)


def solution(mesh):
    in_specs = (
        P(("ctx", "tp"), None),
        P(None, "tp"),
        P(),
        P("tp", None),
        P("tp"),
        P("tp"),
        P("tp"),
        P(None, "tp"),
        P("tp", None),
        P(("ctx", "tp"), None),
    )
    out_specs = (P(("ctx", "tp"), None), P(None, "tp"), P("tp", None), P())
    return jax.shard_map(local, mesh=mesh, in_specs=in_specs, out_specs=out_specs, check_vma=False)
```

profile of v0, /device:TPU:4, one launch (start us, length us, event | category | flops | bytes accessed | tf_op | source)
XLA Modules:
  0.0 1343.6 jit_solution(9077498691237861709)
XLA Ops:
  8.7 6.0 rev.53
  14.8 1.3 convert.70
  18.7 1.3 and_reduce_fusion
  20.6 1.4 slice_bitcast_fusion.12
  22.6 6.3 rev.55
  29.0 8.4 rev.49
  37.4 6.3 rev.51
  43.7 1.3 dynamic-slice.21
  45.7 1.3 dynamic-slice.19
  47.0 85.0 %all-gather.7.cloned.1.call-done = bf16[64,4,2048]{2,1,0:T(4,128)(2,1)} async-done(((bf16[1,4,2048]{2,1,0:T(4,128)(2,1)}), bf16[64,4,2048]{2,1,0:T(4,128)(2,1)}) %all-gather.7.cloned.1.call-update) | async-done | bytes 1048592 | tf_op jit(solution)/shard_map/all_gather | solution.py:119
  132.1 1.3 reshape.271
  138.8 2.1 slice_dynamic-update-slice_fusion
  141.6 107.5 %all-gather.5.cloned.1.call-done = bf16[64,4,2048]{2,1,0:T(4,128)(2,1)} async-done(((bf16[1,4,2048]{2,1,0:T(4,128)(2,1)}), bf16[64,4,2048]{2,1,0:T(4,128)(2,1)}) %all-gather.5.cloned.1.call-update) | async-done | bytes 1048592 | tf_op jit(solution)/shard_map/all_gather | solution.py:150
  249.2 1.3 reshape.269
  250.5 1.5 convolution_bitcast_fusion.2
  253.1 8.6 collective-permute-start
  261.7 1.3 collective-permute-start.1
  263.8 0.9 convolution_add_fusion.9
  264.7 68.7 %all_gather.29 = f32[8,64,16]{1,2,0:T(8,128)S(1)} all-gather(f32[1,64,16]{1,2,0:T(8,128)S(1)} %get-tuple-element.678), channel_id=1, replica_groups=mesh['ctx'=8,'tp'=64] {'ctx'}, dimensions={0}, use_global_device_ids=true | all-gather | bytes 36864 | tf_op jit(solution)/shard_map/all_gather | solution.py:27
  333.4 41.5 %all-reduce.19 = (f32[8]{0:T(128)S(1)}, f32[8]{0:T(128)S(1)}) all-reduce(f32[8]{0:T(128)} %slice_dynamic-update-slice_fusion, f32[8]{0:T(128)} %copy-done.65), channel_id=1, replica_groups=mesh['ctx'=8,'tp'=64] {'ctx'}, use_global_device_ids=true, to_apply=%add.17 | all-reduce | flops 16 | bytes 128
  374.9 10.2 while.62
  385.1 63.2 %all_gather.31 = f32[8,64,16]{1,2,0:T(8,128)S(1)} all-gather(f32[1,64,16]{1,2,0:T(8,128)S(1)} %get-tuple-element.679), channel_id=1, replica_groups=mesh['ctx'=8,'tp'=64] {'ctx'}, dimensions={0}, use_global_device_ids=true | all-gather | bytes 36864 | tf_op jit(solution)/shard_map/all_gather | solution.py:27
  448.3 10.1 while.63
  459.6 0.9 multiply_reduce_fusion.5
  461.9 63.1 %all_gather.32 = f32[8,64,16]{1,2,0:T(8,128)S(1)} all-gather(f32[1,64,16]{1,2,0:T(8,128)S(1)} %get-tuple-element.676), channel_id=1, replica_groups=mesh['ctx'=8,'tp'=64] {'ctx'}, dimensions={0}, use_global_device_ids=true | all-gather | bytes 36864 | tf_op jit(solution)/shard_map/all_gather | solution.py:27
  525.1 10.1 while.64
  535.2 63.3 %all_gather.33 = f32[8,64,16]{1,2,0:T(8,128)S(1)} all-gather(f32[1,64,16]{1,2,0:T(8,128)S(1)} %get-tuple-element.677), channel_id=1, replica_groups=mesh['ctx'=8,'tp'=64] {'ctx'}, dimensions={0}, use_global_device_ids=true | all-gather | bytes 36864 | tf_op jit(solution)/shard_map/all_gather | solution.py:27
  598.4 10.2 while.65
  609.9 1.3 fusion.101
  611.2 1.3 fusion.92
  612.6 1.3 fusion.23
  613.9 1.2 convolution_add_fusion.7
  615.1 1.6 fusion.127
  616.6 1.3 fusion.26
  618.7 1.4 multiply_reduce_fusion.3
  621.3 1.3 copy.40
  622.6 1.3 copy.38
  625.4 1.4 convolution_add_fusion.8
  626.9 1.0 convolution_add_fusion.6
  627.8 2.1 fusion.188
  631.5 2.5 reduce-window.24
  634.9 2.5 reduce-window.26
  639.1 1.1 fusion.112
  640.2 1.3 rev.63
  642.6 0.8 slice.317
  643.4 2.5 collective-permute-start.2
  645.9 1.5 collective-permute-start.3
  648.1 1.1 convolution_bitcast_fusion.1
  649.3 1.9 add_select_fusion
  651.2 2.0 scatter-add.6
  653.2 7.6 collective-permute-done.3
  660.8 1.1 scatter-add.9
  662.0 1.2 convolution_bitcast_fusion
  663.2 1.0 slice.386
  664.2 7.5 rev.61
  671.7 0.9 fusion.10
  672.7 0.8 fusion.157
  673.7 1.2 rev.64
  674.8 1.7 fusion.31
  678.8 453.5 %all-reduce.28 = bf16[256,2048]{1,0:T(8,128)(2,1)S(1)} all-reduce(f32[256,2048]{1,0:T(8,128)S(1)} %fusion.6), channel_id=3, replica_groups=mesh['ctx'=8,'tp'=64] {'tp'}, use_global_device_ids=true, to_apply=%region_27.28.clone | all-reduce | flops 524288 | bytes 3145728
  1133.0 2.2 copy.41
  1135.2 1.8 convert_element_type.39
  1137.0 198.5 %all-reduce.25.cloned.1.call-done = f32[2048,32]{0,1:T(8,128)} async-done(((f32[2048,32]{0,1:T(8,128)}), f32[2048,32]{0,1:T(8,128)}) %all-reduce.25.cloned.1.call-update) | async-done | bytes 262160 | tf_op jit(solution)/shard_map/psum | solution.py:203
  1335.4 1.7 copy.111
  (305 shorter events, 66.8 us)
Async XLA Ops:
  7.2 126.2 %copy-start.27 = (bf16[1,2048]{1,0:T(2,128)(2,1)S(1)}, bf16[1,2048]{1,0:T(2,128)(2,1)}, u32[]{:S(2)}) copy-start(bf16[1,2048]{1,0:T(2,128)(2,1)} %param.25) | copy-start | bytes 12292
  7.2 124.9 %all-gather.7.cloned.1.call-start = ((), (), s32[]{:S(2)}) async-start(), calls=%async_computation.2 | async-start | bytes 1064960 | tf_op jit(solution)/shard_map/all_gather | solution.py:119
  7.9 241.2 %all-gather.5.cloned.1.call-start = ((), (), s32[]{:S(2)}) async-start(), calls=%async_computation.1 | async-start | bytes 1064960 | tf_op jit(solution)/shard_map/all_gather | solution.py:150
  8.7 1124.3 %all-reduce.27.cloned.1.call-start = ((), (), s32[]{:S(2)}) async-start(), calls=%async_computation.3 | async-start | bytes 1572864 | tf_op jit(solution)/shard_map/psum | solution.py:199
  29.0 106.7 %copy-start.5 = (bf16[2048,32]{0,1:T(8,128)(2,1)}, bf16[2048,32]{0,1:T(8,128)(2,1)S(1)}, u32[]{:S(2)}) copy-start(bf16[2048,32]{0,1:T(8,128)(2,1)S(1)} %rev.55) | copy-start | bytes 393220
  37.4 98.3 %copy-start.4 = (bf16[2048,32]{0,1:T(8,128)(2,1)S(1)}, bf16[2048,32]{0,1:T(8,128)(2,1)}, u32[]{:S(2)}) copy-start(bf16[2048,32]{0,1:T(8,128)(2,1)} %param.24) | copy-start | bytes 393220
  43.7 208.6 %copy-start.2 = (bf16[2048,128]{1,0:T(8,128)(2,1)}, bf16[2048,128]{1,0:T(8,128)(2,1)S(1)}, u32[]{:S(2)}) copy-start(bf16[2048,128]{1,0:T(8,128)(2,1)S(1)} %rev.51) | copy-start | bytes 1572868
  134.6 326.7 %copy-start.33 = (f32[256,1]{0,1:T(1,128)}, f32[256,1]{0,1:T(1,128)S(1)}, u32[]{:S(2)}) copy-start(f32[256,1]{0,1:T(1,128)S(1)} %rev.54) | copy-start | bytes 3076
  135.6 116.4 %copy-start.48 = (f32[1,2,2,128]{3,1,2,0:T(2,128)}, f32[1,2,2,128]{3,1,2,0:T(2,128)S(1)}, u32[]{:S(2)}) copy-start(f32[1,2,2,128]{3,1,2,0:T(2,128)S(1)} %copy.67) | copy-start | bytes 6148
  137.7 114.4 %copy-start.63 = (f32[2]{0:T(128)}, f32[2]{0:T(128)S(1)}, u32[]{:S(2)}) copy-start(f32[2]{0:T(128)S(1)} %slice_reduce_fusion.3) | copy-start | bytes 28
  141.6 110.5 %copy-start.65 = (f32[8]{0:T(128)}, f32[8]{0:T(128)S(1)}, u32[]{:S(2)}) copy-start(f32[8]{0:T(128)S(1)} %slice_dynamic-update-slice_fusion.1) | copy-start | bytes 100
  141.6 110.6 %copy-start = (bf16[2048,128]{1,0:T(8,128)(2,1)S(1)}, bf16[2048,128]{1,0:T(8,128)(2,1)}, u32[]{:S(2)}) copy-start(bf16[2048,128]{1,0:T(8,128)(2,1)} %param.23) | copy-start | bytes 1572868
  252.1 11.7 copy-start.15
  252.3 12.4 copy-start.14
  252.3 206.2 %copy-start.34 = (f32[1,256]{1,0:T(1,128)S(1)}, f32[1,256]{1,0:T(1,128)}, u32[]{:S(2)}) copy-start(f32[1,256]{1,0:T(1,128)} %get-tuple-element.686) | copy-start | bytes 3076
  252.8 206.3 %copy-start.42 = (f32[64]{0:T(128)S(1)}, f32[64]{0:T(128)}, u32[]{:S(2)}) copy-start(f32[64]{0:T(128)} %get-tuple-element.689) | copy-start | bytes 772
  252.8 206.3 %copy-start.44 = (f32[64]{0:T(128)S(1)}, f32[64]{0:T(128)}, u32[]{:S(2)}) copy-start(f32[64]{0:T(128)} %get-tuple-element.690) | copy-start | bytes 772
  252.8 206.3 %copy-start.46 = (f32[64]{0:T(128)S(1)}, f32[64]{0:T(128)}, u32[]{:S(2)}) copy-start(f32[64]{0:T(128)} %get-tuple-element.691) | copy-start | bytes 772
  252.8 206.3 %copy-start.53 = (f32[64]{0:T(128)S(1)}, f32[64]{0:T(128)}, u32[]{:S(2)}) copy-start(f32[64]{0:T(128)} %get-tuple-element.688) | copy-start | bytes 772
  252.8 206.8 %copy-start.21 = (f32[256,32]{0,1:T(8,128)S(1)}, f32[256,32]{0,1:T(8,128)}, u32[]{:S(2)}) copy-start(f32[256,32]{0,1:T(8,128)} %rev.56) | copy-start | bytes 98308
  252.8 206.8 %copy-start.23 = (f32[1,256,32]{1,2,0:T(8,128)S(1)}, f32[1,256,32]{1,2,0:T(8,128)}, u32[]{:S(2)}) copy-start(f32[1,256,32]{1,2,0:T(8,128)} %get-tuple-element.672) | copy-start | bytes 98308
  252.9 205.7 %copy-start.24 = (bf16[1,256,64]{1,2,0:T(8,128)(2,1)}, bf16[1,256,64]{1,2,0:T(8,128)(2,1)S(1)}, u32[]{:S(2)}) copy-start(bf16[1,256,64]{1,2,0:T(8,128)(2,1)S(1)} %get-tuple-element.658) | copy-start | bytes 98308
  253.1 205.5 %copy-start.18 = (bf16[256,64]{0,1:T(8,128)(2,1)}, bf16[256,64]{0,1:T(8,128)(2,1)S(1)}, u32[]{:S(2)}) copy-start(bf16[256,64]{0,1:T(8,128)(2,1)S(1)} %rev.52) | copy-start | bytes 98308
  253.1 205.4 %collective-permute-start = (bf16[3,128]{0,1:T(8,128)(2,1)S(1)}, bf16[3,128]{0,1:T(8,128)(2,1)S(1)}, u32[]{:S(2)}, u32[]{:S(2)}) collective-permute-start(bf16[3,128]{0,1:T(8,128)(2,1)S(1)} %get-tuple-element.670), channel_id=1, source_target_pairs={{0,64},{64,128},{128,192},{192,256},{256,320},{320,384},{384,448},... | collective-permute-start | bytes 2312 | tf_op jit(solution)/shard_map/ppermute | solution.py:19
  261.7 196.8 %collective-permute-start.1 = (bf16[3,128]{0,1:T(8,128)(2,1)S(1)}, bf16[3,128]{0,1:T(8,128)(2,1)S(1)}, u32[]{:S(2)}, u32[]{:S(2)}) collective-permute-start(bf16[3,128]{0,1:T(8,128)(2,1)S(1)} %get-tuple-element.671), channel_id=1, source_target_pairs={{64,0},{128,64},{192,128},{256,192},{320,256},{384,320},{448,384},... | collective-permute-start | bytes 2312 | tf_op jit(solution)/shard_map/ppermute | solution.py:20
  263.7 196.8 %copy-start.64 = (f32[2]{0:T(128)S(1)}, f32[2]{0:T(128)}, u32[]{:S(2)}) copy-start(f32[2]{0:T(128)} %copy-done.63) | copy-start | bytes 28
  263.7 197.5 %copy-start.35 = (f32[1,256]{1,0:T(1,128)S(1)}, f32[1,256]{1,0:T(1,128)}, u32[]{:S(2)}) copy-start(f32[1,256]{1,0:T(1,128)} %get-tuple-element.686) | copy-start | bytes 3076
  458.5 140.0 %copy-start.36 = (f32[2,256]{1,0:T(2,128)}, f32[2,256]{1,0:T(2,128)S(1)}, u32[]{:S(2)}) copy-start(f32[2,256]{1,0:T(2,128)S(1)} %compare_select_fusion.3) | copy-start | bytes 6148
  459.3 151.9 %copy-start.19 = (bf16[256,64]{0,1:T(8,128)(2,1)S(1)}, bf16[256,64]{0,1:T(8,128)(2,1)}, u32[]{:S(2)}) copy-start(bf16[256,64]{0,1:T(8,128)(2,1)} %copy-done.18) | copy-start | bytes 98308
  459.4 151.9 %copy-start.25 = (bf16[1,256,64]{1,2,0:T(8,128)(2,1)S(1)}, bf16[1,256,64]{1,2,0:T(8,128)(2,1)}, u32[]{:S(2)}) copy-start(bf16[1,256,64]{1,2,0:T(8,128)(2,1)} %copy-done.24) | copy-start | bytes 98308
  460.5 152.1 %copy-start.28 = (pred[256,256]{1,0:T(8,128)(4,1)S(1)}, pred[256,256]{1,0:T(8,128)(4,1)}, u32[]{:S(2)}) copy-start(pred[256,256]{1,0:T(8,128)(4,1)} %iota_compare_fusion) | copy-start | bytes 196612
  460.5 152.1 %copy-start.49 = (f32[1,2,2,128]{3,1,2,0:T(2,128)S(1)}, f32[1,2,2,128]{3,1,2,0:T(2,128)}, u32[]{:S(2)}) copy-start(f32[1,2,2,128]{3,1,2,0:T(2,128)} %copy-done.48) | copy-start | bytes 6148
  609.6 9.0 copy-start.22
  615.1 3.6 copy-start.29
  615.1 3.6 copy-start.37
  615.1 3.6 copy-start.50
  615.1 3.6 copy-start.54
  625.3 4.7 copy-start.39
  625.3 4.7 copy-start.41
  625.4 4.7 copy-start.55
  625.4 4.7 copy-start.56
  625.4 4.7 copy-start.57
  625.4 4.7 copy-start.58
  625.4 4.7 copy-start.59
  625.4 4.7 copy-start.60
  625.4 4.7 copy-start.61
  625.4 4.7 copy-start.62
  626.8 4.2 copy-start.20
  626.8 4.2 copy-start.26
  626.8 4.2 copy-start.67
  627.8 3.4 copy-start.32
  631.0 31.0 %copy-start.7 = (bf16[256,64]{0,1:T(8,128)(2,1)}, bf16[256,64]{0,1:T(8,128)(2,1)S(1)}, u32[]{:S(2)}) copy-start(bf16[256,64]{0,1:T(8,128)(2,1)S(1)} %rev.58) | copy-start | bytes 98308
  631.3 16.8 %copy-start.16 = (bf16[256,32]{0,1:T(8,128)(2,1)}, bf16[256,32]{0,1:T(8,128)(2,1)S(1)}, u32[]{:S(2)}) copy-start(bf16[256,32]{0,1:T(8,128)(2,1)S(1)} %get-tuple-element.674) | copy-start | bytes 49156
  640.2 7.2 copy-start.51
  640.2 7.2 copy-start.52
  643.4 5.8 collective-permute-start.2
  645.9 14.8 %collective-permute-start.3 = (f32[3,64]{0,1:T(8,128)}, f32[3,64]{0,1:T(8,128)S(1)}, u32[]{:S(2)}, u32[]{:S(2)}) collective-permute-start(f32[3,64]{0,1:T(8,128)} %get-tuple-element.638), channel_id=1, source_target_pairs={{64,0},{128,64},{192,128},{256,192},{320,256},{384,320},{448,384},... | collective-permute-start | bytes 2312 | tf_op jit(solution)/shard_map/ppermute | solution.py:20
  672.7 3.9 copy-start.3
  672.7 3.9 copy-start.8
  672.7 3.9 copy-start.12
  672.7 662.7 %all-reduce.25.cloned.1.call-start = ((), (), s32[]{:S(2)}) async-start(), calls=%async_computation | async-start | bytes 524288 | tf_op jit(solution)/shard_map/psum | solution.py:203
  673.6 3.4 copy-start.1
  673.6 3.5 copy-start.10
  673.6 3.5 copy-start.13
  (13 other events, 21.7 us)
Sparse Core Ops, SparseCore 0:
  10.2 121.8 all-gather.6
  134.2 114.9 all-gather.4
  672.8 200.6 all-reduce.26
  879.7 455.7 all-reduce.24
where the time goes:
time: 1350 us; the launch traced here: 1340 us
  blocking collectives  753 us (56%)
  waiting for transfers between devices  400 us (30%)
  local copies, waits for them, and re-layouts  87.5 us (6%)
  other arithmetic  44.4 us (3%)
  matrix products  25.8 us (2%)
  between operations  17.6 us (1%)
  starting transfers between devices  14 us (1%)
    unnamed x2, blocking collectives  495 us
    all_gather x4, blocking collectives, entering(): everything = jax.tree.map(lambda part: lax.all_gather(part, axis), array)  258 us
    psum x1, waiting for transfers between devices, local(): lax.psum((grad_bpair[:, :2 * STATE] + grad_bpair[::-1, 2 * STATE:]) * sca...  198 us
    all_gather x1, waiting for transfers between devices, local(): portion = lax.all_gather(d_out, 'tp', axis=0, tiled=True)  108 us
    all_gather x1, waiting for transfers between devices, local(): gathered = lax.all_gather(hidden, 'tp', axis=0, tiled=True)  85 us
  transfers between devices with their start and end apart: 8, of which 4 were waited for; matrix products, arithmetic and copies ran while one was open for 6% of the time, Pallas kernels for 0%

commit v1 on v0

--- a/solution.py
+++ b/solution.py
@@ -116,7 +116,8 @@
     dt_pair = jnp.concatenate([w_dt, w_dt[:, ::-1]], axis=0)
     out_pair = jnp.concatenate([w_out, w_out[:, ::-1]], axis=0)
     params = (dt_bias[0], -jnp.exp(a_log[0]), d_skip[0], conv_w)
-    gathered = lax.all_gather(hidden, "tp", axis=0, tiled=True)
+    repeated = jnp.stack([hidden] * lax.axis_size("tp"))
+    gathered = jnp.concatenate(lax.all_to_all(repeated, "tp", 0, 0), axis=0)
     projected = jnp.dot(gathered, w_pair, preferred_element_type=jnp.float32).astype(jnp.bfloat16)
     dt_raw = times_rows(gathered, dt_pair)
     b_c_all = jnp.dot(gathered, bc_pair, preferred_element_type=jnp.float32)

time: 1350 us -> 1260 us (0.933)
  waiting for transfers between devices: 400 us -> 311 us
  starting transfers between devices: 14 us -> 31.3 us
  local copies, waits for them, and re-layouts: 87.5 us -> 70.4 us
    all_gather x1 -> x0, waiting for transfers between devices: 85 us -> none  [local(): gathered = lax.all_gather(hidden, 'tp', axis=0, tiled=True)]
    all_to_all x0 -> x1, starting transfers between devices: none -> 16.3 us  [local(): gathered = jnp.concatenate(lax.all_to_all(repeated, 'tp', 0, 0), axis=0)]
  transfers between devices with their start and end apart: 8 -> 8, of which waited for: 4 -> 3; matrix products, arithmetic and copies ran while one was open for 6% -> 4% of each run, Pallas kernels for 0% -> 0%
where the time goes in v1:
time: 1260 us; the launch traced here: 1250 us
  blocking collectives  755 us (60%)
  waiting for transfers between devices  311 us (25%)
  local copies, waits for them, and re-layouts  70.4 us (6%)
  other arithmetic  43 us (3%)
  starting transfers between devices  31.3 us (2%)
  matrix products  24.8 us (2%)
  between operations  17.6 us (1%)
    unnamed x2, blocking collectives  496 us
    all_gather x4, blocking collectives, entering(): everything = jax.tree.map(lambda part: lax.all_gather(part, axis), array)  259 us
    psum x1, waiting for transfers between devices, local(): lax.psum((grad_bpair[:, :2 * STATE] + grad_bpair[::-1, 2 * STATE:]) * sca...  199 us
    all_gather x1, waiting for transfers between devices, local(): portion = lax.all_gather(d_out, 'tp', axis=0, tiled=True)  104 us
  transfers between devices with their start and end apart: 8, of which 3 were waited for; matrix products, arithmetic and copies ran while one was open for 4% of the time, Pallas kernels for 0%

profile of v1, /device:TPU:4, one launch (start us, length us, event | category | flops | bytes accessed | tf_op | source)
XLA Modules:
  0.0 1253.9 jit_solution(16959894106469017364)
XLA Ops:
  7.2 2.3 stack.55
  9.5 16.3 %all-to-all-start = ((bf16[64,4,2048]{2,1,0:T(4,128)(2,1)}), bf16[64,4,2048]{2,1,0:T(4,128)(2,1)S(1)}, u32[]{:S(2)}, u32[]{:S(2)}) async-start(bf16[64,4,2048]{2,1,0:T(4,128)(2,1)} %stack.55), calls=%async_computation | async-start | bytes 2097152 | tf_op jit(solution)/shard_map/all_to_all | solution.py:120
  26.6 1.5 rev.53
  31.2 1.3 rev.55
  32.6 1.4 rev.49
  34.0 5.1 rev.51
  39.1 1.3 dynamic-slice.21
  41.0 1.3 dynamic-slice.19
  44.8 103.7 %all-gather.3.cloned.1.call-done = bf16[64,4,2048]{2,1,0:T(4,128)(2,1)} async-done(((bf16[1,4,2048]{2,1,0:T(4,128)(2,1)}), bf16[64,4,2048]{2,1,0:T(4,128)(2,1)}) %all-gather.3.cloned.1.call-update) | async-done | bytes 1048592 | tf_op jit(solution)/shard_map/all_gather | solution.py:151
  148.5 1.3 reshape.275
  154.8 1.9 slice_dynamic-update-slice_fusion
  159.6 8.7 collective-permute-start
  168.3 1.3 collective-permute-start.1
  170.4 0.8 convolution_add_fusion.9
  171.2 69.2 %all_gather.25 = f32[8,64,16]{1,2,0:T(8,128)S(1)} all-gather(f32[1,64,16]{1,2,0:T(8,128)S(1)} %get-tuple-element.678), channel_id=1, replica_groups=mesh['ctx'=8,'tp'=64] {'ctx'}, dimensions={0}, use_global_device_ids=true | all-gather | bytes 36864 | tf_op jit(solution)/shard_map/all_gather | solution.py:27
  240.5 40.7 %all-reduce.19 = (f32[8]{0:T(128)S(1)}, f32[8]{0:T(128)S(1)}) all-reduce(f32[8]{0:T(128)} %slice_dynamic-update-slice_fusion, f32[8]{0:T(128)} %copy-done.69), channel_id=1, replica_groups=mesh['ctx'=8,'tp'=64] {'ctx'}, use_global_device_ids=true, to_apply=%add.17 | all-reduce | flops 16 | bytes 128
  281.1 10.0 while.62
  291.1 63.1 %all_gather.27 = f32[8,64,16]{1,2,0:T(8,128)S(1)} all-gather(f32[1,64,16]{1,2,0:T(8,128)S(1)} %get-tuple-element.679), channel_id=1, replica_groups=mesh['ctx'=8,'tp'=64] {'ctx'}, dimensions={0}, use_global_device_ids=true | all-gather | bytes 36864 | tf_op jit(solution)/shard_map/all_gather | solution.py:27
  354.2 10.8 while.63
  366.2 0.9 multiply_reduce_fusion.5
  367.0 0.8 multiply_reduce_fusion.9
  368.5 63.1 %all_gather.28 = f32[8,64,16]{1,2,0:T(8,128)S(1)} all-gather(f32[1,64,16]{1,2,0:T(8,128)S(1)} %get-tuple-element.676), channel_id=1, replica_groups=mesh['ctx'=8,'tp'=64] {'ctx'}, dimensions={0}, use_global_device_ids=true | all-gather | bytes 36864 | tf_op jit(solution)/shard_map/all_gather | solution.py:27
  431.5 10.1 while.64
  441.7 63.3 %all_gather.29 = f32[8,64,16]{1,2,0:T(8,128)S(1)} all-gather(f32[1,64,16]{1,2,0:T(8,128)S(1)} %get-tuple-element.677), channel_id=1, replica_groups=mesh['ctx'=8,'tp'=64] {'ctx'}, dimensions={0}, use_global_device_ids=true | all-gather | bytes 36864 | tf_op jit(solution)/shard_map/all_gather | solution.py:27
  504.9 10.2 while.65
  516.3 1.3 fusion.101
  517.7 1.3 fusion.92
  519.0 1.3 fusion.23
  520.4 1.2 convolution_add_fusion.7
  521.5 1.6 fusion.127
  523.1 1.3 fusion.26
  525.1 1.4 multiply_reduce_fusion.3
  526.6 0.8 add_bitcast_fusion
  527.8 1.3 copy.40
  529.1 1.3 copy.38
  531.9 1.4 convolution_add_fusion.8
  533.3 1.0 convolution_add_fusion.6
  534.3 2.1 fusion.188
  537.9 2.5 reduce-window.24
  541.4 2.5 reduce-window.26
  544.8 0.8 rev.62
  545.6 1.1 fusion.112
  546.8 1.3 rev.63
  548.1 0.8 fusion.15
  549.1 0.8 slice.317
  549.9 3.4 collective-permute-start.2
  553.4 1.5 collective-permute-start.3
  555.6 1.1 convolution_bitcast_fusion.1
  556.7 2.0 add_select_fusion
  558.7 2.1 scatter-add.6
  560.8 7.4 collective-permute-done.3
  568.3 1.1 scatter-add.9
  569.4 1.2 convolution_bitcast_fusion
  570.6 1.0 slice.386
  571.7 7.5 rev.61
  579.2 0.9 fusion.10
  580.2 0.8 fusion.157
  581.1 1.2 rev.64
  582.3 1.7 fusion.31
  586.3 455.7 %all-reduce.28 = bf16[256,2048]{1,0:T(8,128)(2,1)S(1)} all-reduce(f32[256,2048]{1,0:T(8,128)S(1)} %fusion.6), channel_id=3, replica_groups=mesh['ctx'=8,'tp'=64] {'tp'}, use_global_device_ids=true, to_apply=%region_27.28.clone | all-reduce | flops 524288 | bytes 3145728
  1042.6 2.2 copy.41
  1044.9 1.8 convert_element_type.39
  1046.6 199.1 %all-reduce.25.cloned.1.call-done = f32[2048,32]{0,1:T(8,128)} async-done(((f32[2048,32]{0,1:T(8,128)}), f32[2048,32]{0,1:T(8,128)}) %all-reduce.25.cloned.1.call-update) | async-done | bytes 262160 | tf_op jit(solution)/shard_map/psum | solution.py:204
  1245.7 1.7 copy.111
  (315 shorter events, 66.0 us)
Async XLA Ops:
  7.2 19.4 %copy-start.30 = (bf16[1,2048]{1,0:T(2,128)(2,1)S(1)}, bf16[1,2048]{1,0:T(2,128)(2,1)}, u32[]{:S(2)}) copy-start(bf16[1,2048]{1,0:T(2,128)(2,1)} %param.25) | copy-start | bytes 12292
  7.2 24.1 %copy-start.5 = (bf16[2048,32]{0,1:T(8,128)(2,1)S(1)}, bf16[2048,32]{0,1:T(8,128)(2,1)}, u32[]{:S(2)}) copy-start(bf16[2048,32]{0,1:T(8,128)(2,1)} %param.24) | copy-start | bytes 393220
  7.2 25.4 %copy-start.16 = (bf16[64,2048]{1,0:T(8,128)(2,1)S(1)}, bf16[64,2048]{1,0:T(8,128)(2,1)}, u32[]{:S(2)}) copy-start(bf16[64,2048]{1,0:T(8,128)(2,1)} %param.30) | copy-start | bytes 786436
  7.2 26.8 %copy-start = (bf16[2048,128]{1,0:T(8,128)(2,1)S(1)}, bf16[2048,128]{1,0:T(8,128)(2,1)}, u32[]{:S(2)}) copy-start(bf16[2048,128]{1,0:T(8,128)(2,1)} %param.23) | copy-start | bytes 1572868
  9.5 33.4 %copy-start.70 = (s32[2]{0:T(128)S(1)}, s32[2]{0:T(128)}, u32[]{:S(2)}) copy-start(s32[2]{0:T(128)} %constant.218.clone.1) | copy-start | bytes 28
  9.5 34.7 %copy-start.58 = (f32[4,64]{1,0:T(4,128)S(1)}, f32[4,64]{1,0:T(4,128)}, u32[]{:S(2)}) copy-start(f32[4,64]{1,0:T(4,128)} %param.29) | copy-start | bytes 3076
  9.5 141.6 %all-to-all-start = ((bf16[64,4,2048]{2,1,0:T(4,128)(2,1)}), bf16[64,4,2048]{2,1,0:T(4,128)(2,1)S(1)}, u32[]{:S(2)}, u32[]{:S(2)}) async-start(bf16[64,4,2048]{2,1,0:T(4,128)(2,1)} %stack.55), calls=%async_computation | async-start | bytes 2097152 | tf_op jit(solution)/shard_map/all_to_all | solution.py:120
  25.8 122.7 %all-gather.3.cloned.1.call-start = ((), (), s32[]{:S(2)}) async-start(), calls=%async_computation.2 | async-start | bytes 1064960 | tf_op jit(solution)/shard_map/all_gather | solution.py:151
  26.5 1016.1 %all-reduce.27.cloned.1.call-start = ((), (), s32[]{:S(2)}) async-start(), calls=%async_computation.3 | async-start | bytes 1572864 | tf_op jit(solution)/shard_map/psum | solution.py:200
  32.6 124.9 %copy-start.6 = (bf16[2048,32]{0,1:T(8,128)(2,1)}, bf16[2048,32]{0,1:T(8,128)(2,1)S(1)}, u32[]{:S(2)}) copy-start(bf16[2048,32]{0,1:T(8,128)(2,1)S(1)} %rev.55) | copy-start | bytes 393220
  151.1 19.2 %copy-start.15 = (f32[256,64]{0,1:T(8,128)}, f32[256,64]{0,1:T(8,128)S(1)}, u32[]{:S(2)}) copy-start(f32[256,64]{0,1:T(8,128)S(1)} %rev.50) | copy-start | bytes 196612
  151.4 7.3 copy-start.1
  151.4 7.3 copy-start.3
  152.5 215.3 %copy-start.36 = (f32[256,1]{0,1:T(1,128)}, f32[256,1]{0,1:T(1,128)S(1)}, u32[]{:S(2)}) copy-start(f32[256,1]{0,1:T(1,128)S(1)} %rev.54) | copy-start | bytes 3076
  153.6 4.9 copy-start.51
  153.8 5.4 copy-start.67
  157.9 12.4 copy-start.17
  158.7 12.5 copy-start.23
  158.7 206.3 %copy-start.37 = (f32[1,256]{1,0:T(1,128)S(1)}, f32[1,256]{1,0:T(1,128)}, u32[]{:S(2)}) copy-start(f32[1,256]{1,0:T(1,128)} %get-tuple-element.686) | copy-start | bytes 3076
  159.2 206.4 %copy-start.45 = (f32[64]{0:T(128)S(1)}, f32[64]{0:T(128)}, u32[]{:S(2)}) copy-start(f32[64]{0:T(128)} %get-tuple-element.689) | copy-start | bytes 772
  159.2 206.4 %copy-start.47 = (f32[64]{0:T(128)S(1)}, f32[64]{0:T(128)}, u32[]{:S(2)}) copy-start(f32[64]{0:T(128)} %get-tuple-element.690) | copy-start | bytes 772
  159.3 206.4 %copy-start.49 = (f32[64]{0:T(128)S(1)}, f32[64]{0:T(128)}, u32[]{:S(2)}) copy-start(f32[64]{0:T(128)} %get-tuple-element.691) | copy-start | bytes 772
  159.3 206.4 %copy-start.56 = (f32[64]{0:T(128)S(1)}, f32[64]{0:T(128)}, u32[]{:S(2)}) copy-start(f32[64]{0:T(128)} %get-tuple-element.688) | copy-start | bytes 772
  159.3 206.9 %copy-start.26 = (f32[1,256,32]{1,2,0:T(8,128)S(1)}, f32[1,256,32]{1,2,0:T(8,128)}, u32[]{:S(2)}) copy-start(f32[1,256,32]{1,2,0:T(8,128)} %get-tuple-element.672) | copy-start | bytes 98308
  159.3 205.8 %copy-start.27 = (bf16[1,256,64]{1,2,0:T(8,128)(2,1)}, bf16[1,256,64]{1,2,0:T(8,128)(2,1)S(1)}, u32[]{:S(2)}) copy-start(bf16[1,256,64]{1,2,0:T(8,128)(2,1)S(1)} %get-tuple-element.658) | copy-start | bytes 98308
  159.5 205.8 %copy-start.20 = (bf16[256,64]{0,1:T(8,128)(2,1)}, bf16[256,64]{0,1:T(8,128)(2,1)S(1)}, u32[]{:S(2)}) copy-start(bf16[256,64]{0,1:T(8,128)(2,1)S(1)} %rev.52) | copy-start | bytes 98308
  159.6 205.5 %collective-permute-start = (bf16[3,128]{0,1:T(8,128)(2,1)S(1)}, bf16[3,128]{0,1:T(8,128)(2,1)S(1)}, u32[]{:S(2)}, u32[]{:S(2)}) collective-permute-start(bf16[3,128]{0,1:T(8,128)(2,1)S(1)} %get-tuple-element.670), channel_id=1, source_target_pairs={{0,64},{64,128},{128,192},{192,256},{256,320},{320,384},{384,448},... | collective-permute-start | bytes 2312 | tf_op jit(solution)/shard_map/ppermute | solution.py:19
  168.3 196.8 %collective-permute-start.1 = (bf16[3,128]{0,1:T(8,128)(2,1)S(1)}, bf16[3,128]{0,1:T(8,128)(2,1)S(1)}, u32[]{:S(2)}, u32[]{:S(2)}) collective-permute-start(bf16[3,128]{0,1:T(8,128)(2,1)S(1)} %get-tuple-element.671), channel_id=1, source_target_pairs={{64,0},{128,64},{192,128},{256,192},{320,256},{384,320},{448,384},... | collective-permute-start | bytes 2312 | tf_op jit(solution)/shard_map/ppermute | solution.py:20
  170.3 196.7 %copy-start.68 = (f32[2]{0:T(128)S(1)}, f32[2]{0:T(128)}, u32[]{:S(2)}) copy-start(f32[2]{0:T(128)} %copy-done.67) | copy-start | bytes 28
  170.3 197.5 %copy-start.38 = (f32[1,256]{1,0:T(1,128)S(1)}, f32[1,256]{1,0:T(1,128)}, u32[]{:S(2)}) copy-start(f32[1,256]{1,0:T(1,128)} %get-tuple-element.686) | copy-start | bytes 3076
  171.2 194.9 %copy-start.24 = (f32[256,32]{0,1:T(8,128)S(1)}, f32[256,32]{0,1:T(8,128)}, u32[]{:S(2)}) copy-start(f32[256,32]{0,1:T(8,128)} %copy-done.23) | copy-start | bytes 98308
  365.0 139.9 %copy-start.39 = (f32[2,256]{1,0:T(2,128)}, f32[2,256]{1,0:T(2,128)S(1)}, u32[]{:S(2)}) copy-start(f32[2,256]{1,0:T(2,128)S(1)} %compare_select_fusion.3) | copy-start | bytes 6148
  365.9 151.8 %copy-start.21 = (bf16[256,64]{0,1:T(8,128)(2,1)S(1)}, bf16[256,64]{0,1:T(8,128)(2,1)}, u32[]{:S(2)}) copy-start(bf16[256,64]{0,1:T(8,128)(2,1)} %copy-done.20) | copy-start | bytes 98308
  365.9 151.8 %copy-start.28 = (bf16[1,256,64]{1,2,0:T(8,128)(2,1)S(1)}, bf16[1,256,64]{1,2,0:T(8,128)(2,1)}, u32[]{:S(2)}) copy-start(bf16[1,256,64]{1,2,0:T(8,128)(2,1)} %copy-done.27) | copy-start | bytes 98308
  367.0 152.0 %copy-start.31 = (pred[256,256]{1,0:T(8,128)(4,1)S(1)}, pred[256,256]{1,0:T(8,128)(4,1)}, u32[]{:S(2)}) copy-start(pred[256,256]{1,0:T(8,128)(4,1)} %iota_compare_fusion) | copy-start | bytes 196612
  367.0 152.0 %copy-start.52 = (f32[1,2,2,128]{3,1,2,0:T(2,128)S(1)}, f32[1,2,2,128]{3,1,2,0:T(2,128)}, u32[]{:S(2)}) copy-start(f32[1,2,2,128]{3,1,2,0:T(2,128)} %copy-done.51) | copy-start | bytes 6148
  516.1 9.0 copy-start.25
  521.5 3.6 copy-start.32
  521.5 3.6 copy-start.40
  521.5 3.6 copy-start.53
  521.5 3.6 copy-start.57
  531.8 4.7 copy-start.42
  531.8 4.7 copy-start.44
  531.8 4.7 copy-start.59
  531.8 4.7 copy-start.60
  531.8 4.7 copy-start.61
  531.8 4.7 copy-start.62
  531.8 4.7 copy-start.63
  531.8 4.7 copy-start.64
  531.9 4.7 copy-start.65
  531.9 4.7 copy-start.66
  533.3 4.2 copy-start.22
  533.3 4.2 copy-start.29
  533.3 4.2 copy-start.72
  537.4 32.0 %copy-start.8 = (bf16[256,64]{0,1:T(8,128)(2,1)}, bf16[256,64]{0,1:T(8,128)(2,1)S(1)}, u32[]{:S(2)}) copy-start(bf16[256,64]{0,1:T(8,128)(2,1)S(1)} %rev.58) | copy-start | bytes 98308
  537.7 17.8 %copy-start.18 = (bf16[256,32]{0,1:T(8,128)(2,1)}, bf16[256,32]{0,1:T(8,128)(2,1)S(1)}, u32[]{:S(2)}) copy-start(bf16[256,32]{0,1:T(8,128)(2,1)S(1)} %get-tuple-element.674) | copy-start | bytes 49156
  546.7 8.2 copy-start.54
  546.7 8.2 copy-start.55
  549.9 6.8 collective-permute-start.2
  553.4 14.8 %collective-permute-start.3 = (f32[3,64]{0,1:T(8,128)}, f32[3,64]{0,1:T(8,128)S(1)}, u32[]{:S(2)}, u32[]{:S(2)}) collective-permute-start(f32[3,64]{0,1:T(8,128)} %get-tuple-element.638), channel_id=1, source_target_pairs={{64,0},{128,64},{192,128},{256,192},{320,256},{384,320},{448,384},... | collective-permute-start | bytes 2312 | tf_op jit(solution)/shard_map/ppermute | solution.py:20
  580.1 3.9 copy-start.4
  580.1 3.9 copy-start.9
  580.1 3.9 copy-start.13
  580.1 665.5 %all-reduce.25.cloned.1.call-start = ((), (), s32[]{:S(2)}) async-start(), calls=%async_computation.1 | async-start | bytes 524288 | tf_op jit(solution)/shard_map/psum | solution.py:204
  (18 other events, 37.3 us)
Sparse Core Ops, SparseCore 0:
  28.8 119.6 all-gather.2
  580.3 201.7 all-reduce.26
  788.4 457.2 all-reduce.24
